TPU v7x, 256 devices: a whole 4x4x8 slice. The times are simulated.
256 devices in a mesh: gx: 32 (over z, y_lo, core), gz: 8 (over y_hi, x).
Axes of the slice: x: 4, y: 4 (y_hi: 2, y_lo: 2; y = y_hi * 2 + y_lo), z: 8, core: 2. Of those that a mesh axis runs over, the one named last changes fastest.
Arguments:
- bins: float32 [256, 33, 8, 4096], P('gz', None, None, 'gx'), may hold values from 0.05 to 1
- u_courant: float32 [256, 8, 4096], P('gz', None, 'gx'), may hold values from -0.3 to 0.3
- w_courant: float32 [256, 8, 4096], P('gz', None, 'gx'), may hold values from -0.15 to 0.15
- fall_courant: float32 [33], replicated, may hold values from 0.01 to 0.2
- kernel: float32 [33, 33], replicated, may hold values from 0.005 to 0.05
- redistribution: float32 [33, 33], replicated, may hold values from -1 to 1
- block_ids: int32 [8, 2048], P('gz', 'gx'), may hold values from 0 to 63, as said below
- block_counts: int32 [8, 32], P('gz', 'gx'), may hold values from 1 to 32, 512 in all within a row
- block_inverse: float32 [256, 32, 4096], P('gz', None, 'gx'), may hold values from -0.5 to 0.6
Outputs:
- next_bins: float32 [256, 33, 8, 4096], P('gz', None, None, 'gx')
- pressure: float32 [256, 8, 4096], P('gz', None, 'gx')
Inputs may be any that keep to these rules, and one draw needn't show every extreme that they name: `block_ids`: each device's 64 entries are a permutation of 0 .. 63. `block_counts`: along gx the counts of one gz index sum to exactly 64 * 32 // 4, and one device holds 32.
All inputs are finite; a program needn't handle non-finite values.
Results may differ from a plain program's by a relative error of at most 0.0001.
Values sent between devices are 32-bit elements; how exact they have to be, the bound alone decides.
A program may use at most 128 MiB of HBM per device.

v0:
```python
import functools
import math

import jax
import jax.numpy as jnp
import numpy as np
from jax import lax
from jax.experimental import pallas as pl
from jax.experimental.pallas import tpu as pltpu
from jax.sharding import PartitionSpec as P

F32 = jnp.float32
BF16 = jnp.bfloat16
MESH = pl.DeviceIdType.MESH
NB = 33
NBP = 48
NL = 32
NG = 8
NP = 32
LVL = NB * 8


def halves(x):
    hi = np.asarray(np.asarray(x, np.float32), jnp.bfloat16)
    lo = np.asarray(np.asarray(x - hi.astype(np.float64), np.float32), jnp.bfloat16)
    return hi, lo


def tables():
    p = np.arange(32)
    c = np.arange(128)
    pj = 2.0 * math.pi / 32 * (p[:, None] * c[None, :] % 32)
    cj = 2.0 * math.pi / 4096 * (c[:, None] * c[None, :])
    cos, sin = np.cos(pj), np.sin(pj)
    e_hi, e_lo = halves(np.concatenate([cos, -sin], 1))
    e3 = np.concatenate([e_hi, e_hi, e_lo], 0)
    fwd = np.concatenate([np.concatenate([cos, sin], 1), np.concatenate([-sin, cos], 1)], 0)
    f2 = np.concatenate(halves(fwd), 0)
    g = np.concatenate([np.concatenate([cos, sin], 1), np.concatenate([-sin, cos], 1)], 0)
    g_hi, g_lo = halves(g)
    g3 = np.concatenate([g_hi, g_hi, g_lo], 0)
    h2 = np.concatenate(halves(np.concatenate([cos, -sin], 1) / 4096.0), 0)
    mats = np.concatenate([e3, f2, g3, h2], 0)
    tw = np.concatenate([np.cos(cj), -np.sin(cj)], 1).astype(np.float32)
    return mats, tw


def split(x):
    hi = x.astype(BF16)
    lo = (x - hi.astype(F32)).astype(BF16)
    return hi, lo


def dot(a, b):
    return jnp.dot(a, b, preferred_element_type=F32)


def dot_t(a, b):
    return lax.dot_general(a, b, (((0,), (0,)), ((), ())), preferred_element_type=F32)


def kernel_body(
    bins_h, u_h, w_h, binv_h, mats_h, tw_h, coll_h, ids_v, fall_s, cnt_s,
    out_h, pres_h,
    bins_v, out_v, u_v, w_v, binv_v, mats_v, tw_v, coll_v,
    send1, x1, send2, x2, send3, x3, send4, ybuf,
    esend, edges, csend, corners, bpad, tpad,
    whalo, zlo, zhi, send_f, send_l, send_u, halo_r, halo_l, halo_u, prior,
    adv, fz, mask_v,
    in_sem, bin_sem, out_sem, p_sem,
    a2a_send, a2a_recv, e_send, e_recv, c_send, c_recv, h_send, h_recv,
):
    me = lax.axis_index("gx")
    g = lax.axis_index("gz")
    right = {"gx": lax.rem(me + 1, NP)}
    left = {"gx": lax.rem(me + NP - 1, NP)}
    above = {"gz": lax.rem(g + 1, NG)}
    below = {"gz": lax.rem(g + NG - 1, NG)}

    lane = lax.broadcasted_iota(jnp.int32, (8, 128), 1)
    sub = lax.broadcasted_iota(jnp.int32, (8, 128), 0)

    barrier = pltpu.get_barrier_semaphore()

    def greet_x(o, _):
        pl.semaphore_signal(barrier, inc=1, device_id={"gx": lax.rem(me + o, NP)}, device_id_type=MESH)
        return 0

    def greet_z(o, _):
        pl.semaphore_signal(barrier, inc=1, device_id={"gz": lax.rem(g + o, NG)}, device_id_type=MESH)
        return 0

    lax.fori_loop(1, NP, greet_x, 0)
    lax.fori_loop(1, NG, greet_z, 0)

    loads = [
        pltpu.make_async_copy(s, d, in_sem.at[i])
        for i, (s, d) in enumerate(
            [(u_h, u_v), (w_h, w_v), (binv_h, binv_v), (mats_h, mats_v), (tw_h, tw_v), (coll_h, coll_v)]
        )
    ]
    loads[0].start()
    loads[1].start()
    bin_loads = [
        pltpu.make_async_copy(bins_h.at[pl.ds(i * 4 * LVL, 4 * LVL)], bins_v.at[pl.ds(i * 4 * LVL, 4 * LVL)], bin_sem.at[i])
        for i in range(8)
    ]
    for i in range(8):
        bin_loads[i].start()
    for c in loads[2:]:
        c.start()
    loads[0].wait()
    loads[1].wait()

    def tile_div(q, w_under):
        u = u_v[pl.ds(q * 8, 8), :]
        before = jnp.where(lane == 0, 0.0, pltpu.roll(u, 1, 1))
        d = (u - before) + (w_v[pl.ds(q * 8, 8), :] - w_under)
        row = jnp.sum(jnp.where(lane == sub, jnp.broadcast_to(u[:, 127:128], (8, 128)), 0.0), axis=0, keepdims=True)
        send1[pl.ds(q * 16, 8), :] = d
        send1[pl.ds(q * 16 + 8, 8), :] = jnp.broadcast_to(row, (8, 128))

    tile_div(0, jnp.zeros((8, 128), F32))

    def div_step(q, _):
        tile_div(q, w_v[pl.ds(q * 8 - 8, 8), :])
        return 0

    lax.fori_loop(1, NL, div_step, 0)

    pl.semaphore_wait(barrier, NP - 1 + NG - 1)

    w_copy = pltpu.make_async_remote_copy(
        src_ref=w_v.at[pl.ds(248, 8)], dst_ref=whalo, send_sem=h_send.at[0], recv_sem=h_recv.at[0],
        device_id=above, device_id_type=MESH)
    w_copy.start()

    def msg(stage, src, dst, rows, peer, at):
        s0 = pl.multiple_of(peer * at, 8)
        d0 = pl.multiple_of(me * at, 8)
        return pltpu.make_async_remote_copy(
            src_ref=src.at[pl.ds(s0, rows)], dst_ref=dst.at[pl.ds(d0, rows)],
            send_sem=a2a_send.at[stage, peer], recv_sem=a2a_recv.at[stage, me],
            device_id={"gx": peer}, device_id_type=MESH)

    def peer_of(t):
        half = (t + 1) // 2
        odd = lax.rem(t, 2)
        o = 16 + odd * half - (1 - odd) * half
        return lax.rem(me + o, NP)

    def send_all(stage, src, dst, rows, at, skip=False):
        def step(t, _):
            peer = peer_of(t)
            if skip:
                @pl.when(peer != 0)
                def _():
                    msg(stage, src, dst, rows, peer, at).start()
            else:
                msg(stage, src, dst, rows, peer, at).start()
            return 0
        lax.fori_loop(0, NP - 1, step, 0)

    def wait_all(stage, src, dst, rows, at):
        def step(t, _):
            peer = lax.rem(me + t + 1, NP)
            d0 = pl.multiple_of(peer * at, 8)
            pltpu.make_async_remote_copy(
                src_ref=src.at[pl.ds(d0, rows)], dst_ref=dst.at[pl.ds(d0, rows)],
                send_sem=a2a_send.at[stage, peer], recv_sem=a2a_recv.at[stage, peer],
                device_id={"gx": peer}, device_id_type=MESH).wait()
            return 0
        lax.fori_loop(0, NP - 1, step, 0)

    def own(src, dst, rows, at):
        m0 = pl.multiple_of(me * at, 8)
        dst[pl.ds(m0, rows), :] = src[pl.ds(m0, rows), :]

    send_all(0, send1, x1, 9, 16, skip=True)

    bin_loads[7].wait()
    bin_loads[0].wait()
    z_up = pltpu.make_async_remote_copy(
        src_ref=bins_v.at[pl.ds(31 * LVL, LVL)], dst_ref=zlo, send_sem=h_send.at[1], recv_sem=h_recv.at[1],
        device_id=above, device_id_type=MESH)
    z_down = pltpu.make_async_remote_copy(
        src_ref=bins_v.at[pl.ds(0, LVL)], dst_ref=zhi, send_sem=h_send.at[2], recv_sem=h_recv.at[2],
        device_id=below, device_id_type=MESH)
    z_up.start()
    z_down.start()

    w_copy.wait()
    not_first = g > 0
    send1[pl.ds(0, 8), :] = send1[pl.ds(0, 8), :] - jnp.where(not_first, whalo[...], 0.0)

    @pl.when(me != 0)
    def _():
        msg(0, send1, x1, 9, me * 0, 16).start()

    own(send1, x1, 16, 16)

    loads[2].wait()
    csend[...] = jnp.zeros((8, 128), F32)
    for i, r in enumerate((0, 31, 31 * 32, 31 * 32 + 31)):
        csend[pl.ds(i, 1), :] = binv_v[pl.ds(r, 1), :]

    def z_msg(src, dst, rows, peer, ss, rs):
        d0 = pl.multiple_of(g * rows, 8)
        return pltpu.make_async_remote_copy(
            src_ref=src, dst_ref=dst.at[pl.ds(d0, rows)], send_sem=ss.at[peer], recv_sem=rs.at[g],
            device_id={"gz": peer}, device_id_type=MESH)

    def send_z(src, dst, rows, ss, rs):
        def step(o, _):
            z_msg(src, dst, rows, lax.rem(g + o, NG), ss, rs).start()
            return 0
        lax.fori_loop(1, NG, step, 0)
        dst[pl.ds(pl.multiple_of(g * rows, 8), rows), :] = src[...]

    def wait_z(src, dst, rows, ss, rs):
        def step(o, _):
            peer = lax.rem(g + o, NG)
            pltpu.make_async_remote_copy(
                src_ref=src, dst_ref=dst.at[pl.ds(pl.multiple_of(peer * rows, 8), rows)], send_sem=ss.at[peer], recv_sem=rs.at[peer],
                device_id={"gz": peer}, device_id_type=MESH).wait()
            return 0
        lax.fori_loop(1, NG, step, 0)

    send_z(csend, corners, 8, c_send, c_recv)

    for i in range(1, 7):
        bin_loads[i].wait()

    def pack(i, _):
        first = jnp.zeros((8, 128), F32)
        last = jnp.zeros((8, 128), F32)
        for r in range(2):
            for m in range(NB):
                v = bins_v[pl.ds((2 * i + r) * LVL + m * 8, 8), :]
                hit = lane == (NB * r + m)
                first = jnp.where(hit, jnp.broadcast_to(v[:, 0:1], (8, 128)), first)
                last = jnp.where(hit, jnp.broadcast_to(v[:, 127:128], (8, 128)), last)
        speeds = jnp.where(
            lane < NB,
            jnp.broadcast_to(u_v[pl.ds(i * 16, 8), :][:, 127:128], (8, 128)),
            jnp.broadcast_to(u_v[pl.ds(i * 16 + 8, 8), :][:, 127:128], (8, 128)))
        send_f[pl.ds(i * 8, 8), :] = first
        send_l[pl.ds(i * 8, 8), :] = last
        send_u[pl.ds(i * 8, 8), :] = speeds
        return 0

    lax.fori_loop(0, NL // 2, pack, 0)
    x_copies = [
        pltpu.make_async_remote_copy(src_ref=s, dst_ref=d, send_sem=h_send.at[i], recv_sem=h_recv.at[i], device_id=to, device_id_type=MESH)
        for i, s, d, to in ((3, send_f, halo_r, left), (4, send_l, halo_l, right), (5, send_u, halo_u, right))
    ]
    for c in x_copies:
        c.start()

    block = lax.broadcasted_iota(jnp.int32, (64, 64), 0)
    slot = lax.broadcasted_iota(jnp.int32, (64, 64), 1)
    hits = (jnp.broadcast_to(ids_v[...], (64, 64)) == block) & (slot < cnt_s[0, 0])
    marks = jnp.max(jnp.where(hits, 1.0, 0.0), axis=1, keepdims=True)
    col_block = lax.broadcasted_iota(jnp.int32, (16, 128), 1) // 8
    row_block = lax.broadcasted_iota(jnp.int32, (16, 128), 0)
    for bz in range(4):
        wide = jnp.broadcast_to(marks[bz * 16:bz * 16 + 16, :], (16, 128))
        mask_v[pl.ds(bz, 1), :] = jnp.sum(jnp.where(col_block == row_block, wide, 0.0), axis=0, keepdims=True)

    adv[...] = jnp.zeros((NBP * 8, 128), F32)
    for c in loads[3:]:
        c.wait()

    z_up.wait()
    z_down.wait()
    for c in x_copies:
        c.wait()

    def prior_step(i, _):
        s = pl.ds(i * 8, 8)
        speed = halo_u[s, :]
        prior[s, :] = jnp.maximum(speed, 0.0) * halo_l[s, :] + jnp.minimum(speed, 0.0) * send_f[s, :]
        return 0

    lax.fori_loop(0, NL // 2, prior_step, 0)

    not_last = g < NG - 1
    w_low = jnp.where(not_first, whalo[...], 0.0)

    def low_face(m, _):
        s = pl.ds(m * 8, 8)
        c = w_low - fall_s[m]
        fz[s, :] = jnp.maximum(c, 0.0) * jnp.where(not_first, zlo[s, :], 0.0) + jnp.minimum(c, 0.0) * bins_v[s, :]
        bins_v[pl.ds(NL * LVL + m * 8, 8), :] = jnp.where(not_last, zhi[s, :], 0.0)
        return 0

    lax.fori_loop(0, NB, low_face, 0)

    def level(z, i, r):
        u = u_v[pl.ds(z * 8, 8), :]
        u_pos, u_neg = jnp.maximum(u, 0.0), jnp.minimum(u, 0.0)
        w = w_v[pl.ds(z * 8, 8), :]
        hr = halo_r[pl.ds(i * 8, 8), :]
        pf = prior[pl.ds(i * 8, 8), :]
        base = z * LVL
        for m in range(NB):
            k = NB * r + m
            b = bins_v[pl.ds(base + m * 8, 8), :]
            up = bins_v[pl.ds(base + LVL + m * 8, 8), :]
            nxt = jnp.where(lane == 127, jnp.broadcast_to(hr[:, k:k + 1], (8, 128)), pltpu.roll(b, 127, 1))
            flux = u_pos * b + u_neg * nxt
            prev = jnp.where(lane == 0, jnp.broadcast_to(pf[:, k:k + 1], (8, 128)), pltpu.roll(flux, 1, 1))
            c = w - fall_s[m]
            top = jnp.maximum(c, 0.0) * b + jnp.minimum(c, 0.0) * up
            s = pl.ds(m * 8, 8)
            adv[s, :] = b - (flux - prev) - (top - fz[s, :])
            fz[s, :] = top
        mark = jnp.broadcast_to(mask_v[pl.ds(z // 8, 1), :], (NBP, 128))
        grow_w = coll_v[pl.ds(0, NBP), :]
        redi_w = coll_v[pl.ds(NBP, NBP), :]
        for h in range(4):
            ys = (2 * h, 2 * h + 1)
            v = jnp.concatenate([adv[pl.ds(y, NBP, stride=8), :] for y in ys], axis=1)
            hi, lo = split(v)
            rate = dot(grow_w, jnp.concatenate([hi, hi, lo], axis=0))
            hi, lo = split(v * rate)
            tend = dot(redi_w, jnp.concatenate([hi, hi, lo], axis=0))
            for n, y in enumerate(ys):
                part = slice(128 * n, 128 * n + 128)
                new = v[:, part] + tend[:, part] * mark
                out_v[pl.ds(base + y, NB, stride=8), :] = new[:NB]

    def flush(z2):
        s = pl.ds(z2 * 2 * LVL, 2 * LVL)
        return pltpu.make_async_copy(out_v.at[s], out_h.at[s], out_sem.at[z2])

    def levels(first, last):
        def step(i, _):
            level(2 * i, i, 0)
            level(2 * i + 1, i, 1)
            flush(i).start()
            return 0
        lax.fori_loop(first, last, step, 0)

    levels(0, CUT[0])

    wait_all(0, send1, x1, 9, 16)
    borders = x1[pl.ds(8, NP, stride=16), :]
    borders = pltpu.roll(borders, 1, 0)
    lane32 = lax.broadcasted_iota(jnp.int32, (32, 128), 1)
    e3 = mats_v[pl.ds(0, 96), :]
    f2 = mats_v[pl.ds(96, 128), :]
    twr = tw_v[:, 0:128]
    twi = tw_v[:, 128:256]
    for h in range(4):
        us = []
        for y in (2 * h, 2 * h + 1):
            xy = x1[pl.ds(y, NP, stride=16), :]
            shifted = borders if y == 0 else pltpu.roll(borders, 128 - y, 1)
            xy = xy - jnp.where(lane32 == 0, shifted, 0.0)
            hi, lo = split(xy)
            yy = dot_t(jnp.concatenate([hi, lo, hi], axis=0), e3)
            yr, yi = yy[:, :128], yy[:, 128:]
            us.append(jnp.concatenate([yr * twr - yi * twi, yr * twi + yi * twr], axis=0))
        hi, lo = split(jnp.concatenate(us, axis=1))
        both = dot(f2, hi)
        spec = both[:64] + both[64:] + dot(f2[:64], lo)
        for n, y in enumerate((2 * h, 2 * h + 1)):
            part = slice(128 * n, 128 * n + 128)
            send2[pl.ds(y, NP, stride=16), :] = spec[:32, part]
            send2[pl.ds(8 + y, NP, stride=16), :] = spec[32:, part]
    send_all(1, send2, x2, 16, 16)
    own(send2, x2, 16, 16)

    levels(CUT[0], CUT[1])

    wait_all(1, send2, x2, 16, 16)

    def apply_rows(rows):
        accs = [None] * len(rows)
        for j in range(NL):
            s = x2[pl.ds(j * 16, 16), :]
            for n, i in enumerate(rows):
                b = jnp.broadcast_to(binv_v[pl.ds(i * 32 + j, 1), :], (16, 128))
                accs[n] = b * s if accs[n] is None else accs[n] + b * s
        return accs

    low, high = apply_rows((0, 31))
    esend[pl.ds(0, 16), :] = low
    esend[pl.ds(16, 16), :] = high
    send_z(esend, edges, 32, e_send, e_recv)

    def solve_step(t, _):
        rows = [t * 4 + n for n in range(4)]
        for i, acc in zip(rows, apply_rows(rows)):
            send3[pl.ds(i * 16, 16), :] = acc
        return 0

    lax.fori_loop(0, NL // 4, solve_step, 0)
    wait_z(csend, corners, 8, c_send, c_recv)
    wait_z(esend, edges, 32, e_send, e_recv)

    zero = jnp.zeros((16, 128), F32)
    e0 = [edges[pl.ds(k * 32, 16), :] for k in range(NG)]
    e1 = [edges[pl.ds(k * 32 + 16, 16), :] for k in range(NG)]

    def corner(k, i):
        return jnp.broadcast_to(corners[pl.ds(k * 8 + i, 1), :], (16, 128))

    bs, ts = e0, e1
    for _ in range(2):
        nb, nt = [], []
        for k in range(NG):
            over = bs[k + 1] if k < NG - 1 else zero
            under = ts[k - 1] if k > 0 else zero
            nb.append(e0[k] + corner(k, 1) * over + corner(k, 0) * under)
            nt.append(e1[k] + corner(k, 3) * over + corner(k, 2) * under)
        bs, ts = nb, nt
    for k in range(NG):
        bpad[pl.ds(k * 16, 16), :] = bs[k]
        tpad[pl.ds(k * 16 + 16, 16), :] = ts[k]
    bpad[pl.ds(NG * 16, 16), :] = zero
    tpad[pl.ds(0, 16), :] = zero
    over = bpad[pl.ds(pl.multiple_of(g * 16 + 16, 8), 16), :]
    under = tpad[pl.ds(pl.multiple_of(g * 16, 8), 16), :]

    def update(i, _):
        s = pl.ds(i * 16, 16)
        top = jnp.broadcast_to(binv_v[pl.ds(i * 32 + 31, 1), :], (16, 128))
        bot = jnp.broadcast_to(binv_v[pl.ds(i * 32, 1), :], (16, 128))
        send3[s, :] = send3[s, :] + top * over + bot * under
        return 0

    lax.fori_loop(0, NL, update, 0)
    send_all(2, send3, x3, 16, 16)
    own(send3, x3, 16, 16)

    levels(CUT[1], CUT[2])

    wait_all(2, send3, x3, 16, 16)
    g3 = mats_v[pl.ds(224, 192), :]
    h2 = mats_v[pl.ds(416, 64), :]
    for h in range(4):
        zs = []
        for y in (2 * h, 2 * h + 1):
            s2 = jnp.concatenate([x3[pl.ds(y, NP, stride=16), :], x3[pl.ds(8 + y, NP, stride=16), :]], axis=0)
            hi, lo = split(s2)
            vv = dot_t(jnp.concatenate([hi, lo, hi], axis=0), g3)
            vr, vi = vv[:, :128], vv[:, 128:]
            zs.append(jnp.concatenate([vr * twr + vi * twi, vi * twr - vr * twi], axis=0))
        hi, lo = split(jnp.concatenate(zs, axis=1))
        both = dot(h2, hi)
        pr = both[:32] + both[32:] + dot(h2[:32], lo)
        for n, y in enumerate((2 * h, 2 * h + 1)):
            send4[pl.ds(y, NP, stride=8), :] = pr[:, 128 * n:128 * n + 128]
    send_all(3, send4, pres_h, 8, 8)
    m0 = pl.multiple_of(me * 8, 8)
    own_copy = pltpu.make_async_copy(send4.at[pl.ds(m0, 8)], pres_h.at[pl.ds(m0, 8)], p_sem)
    own_copy.start()

    levels(CUT[2], NL // 2)
    own_copy.wait()

    def drain(i, _):
        flush(i).wait()
        return 0

    lax.fori_loop(0, NL // 2, drain, 0)
    wait_all(3, send4, pres_h, 8, 8)


CUT = (4, 10, 16)


def body(bins, u, w, fall, kern, redi, ids, counts, binv):
    def stacked(m):
        m = jnp.pad(m.T, ((0, NBP - NB), (0, NBP - NB)))
        hi = lax.reduce_precision(m, 8, 7)
        return jnp.concatenate([hi, m - hi, hi], axis=1)

    coll = jnp.concatenate([stacked(kern), stacked(redi)], axis=0).astype(BF16)
    mats, tw = tables()
    vmem = lambda rows, cols=128, t=F32: pltpu.VMEM((rows, cols), t)
    dma = pltpu.SemaphoreType.DMA
    out, pres = pl.pallas_call(
        kernel_body,
        out_shape=(jax.ShapeDtypeStruct((NL * LVL, 128), F32), jax.ShapeDtypeStruct((NL * 8, 128), F32)),
        in_specs=[pl.BlockSpec(memory_space=pl.ANY)] * 7
        + [pl.BlockSpec(memory_space=pltpu.VMEM), pl.BlockSpec(memory_space=pltpu.SMEM), pl.BlockSpec(memory_space=pltpu.SMEM)],
        out_specs=[pl.BlockSpec(memory_space=pl.ANY)] * 2,
        scratch_shapes=[
            vmem((NL + 1) * LVL), vmem(NL * LVL), vmem(256), vmem(256), vmem(1024), vmem(480, 256, BF16), vmem(128, 256), vmem(2 * NBP, 3 * NBP, BF16),
            vmem(512), vmem(512), vmem(512), vmem(512), vmem(512), vmem(512), vmem(256), vmem(8),
            vmem(32), vmem(NG * 32), vmem(8), vmem(NG * 8), vmem((NG + 1) * 16), vmem((NG + 1) * 16),
            vmem(8), vmem(LVL), vmem(LVL), vmem(128), vmem(128), vmem(128), vmem(128), vmem(128), vmem(128), vmem(128),
            vmem(NBP * 8), vmem(LVL), vmem(8),
            dma((6,)), dma((8,)), dma((16,)), dma,
            dma((4, NP)), dma((4, NP)), dma((NG,)), dma((NG,)), dma((NG,)), dma((NG,)), dma((6,)), dma((6,)),
        ],
        compiler_params=pltpu.CompilerParams(collective_id=0, has_side_effects=True, vmem_limit_bytes=60 * 1024 * 1024),
        name="slab_step",
    )(
        bins.reshape(NL * LVL, 128), u.reshape(256, 128), w.reshape(256, 128), binv.reshape(1024, 128),
        jnp.asarray(mats), jnp.asarray(tw), coll, ids, fall, counts,
    )
    return out.reshape(NL, NB, 8, 128), pres.reshape(NL, 8, 128)


def solution(mesh):
    return jax.shard_map(
        body,
        mesh=mesh,
        in_specs=(
            P("gz", None, None, "gx"),
            P("gz", None, "gx"),
            P("gz", None, "gx"),
            P(),
            P(),
            P(),
            P("gz", "gx"),
            P("gz", "gx"),
            P("gz", None, "gx"),
        ),
        out_specs=(P("gz", None, None, "gx"), P("gz", None, "gx")),
        check_vma=False,
    )
```

profile of v0, /device:TPU:1, one launch (start us, length us, event | category | flops | bytes accessed | tf_op | source)
XLA Modules:
  0.0 67.9 jit_solution(15598313898037093308)
XLA Ops:
  1.3 0.8 %copy.13 = f32[33,33]{0,1:T(8,128)S(1)} copy(f32[33,33]{1,0:T(8,128)} %param.15) | data formatting | bytes 8712 | tf_op args[4]
  2.1 0.8 %copy.14 = f32[33,33]{0,1:T(8,128)S(1)} copy(f32[33,33]{1,0:T(8,128)} %param.16) | data formatting | bytes 8712 | tf_op args[5]
  2.9 0.7 %maximum_maximum_fusion.coll_h = bf16[96,144]{1,0:T(8,128)(2,1)} fusion(bf16[48,48]{1,0:T(8,128)(2,1)S(1)} %get-tuple-element.10, bf16[48,48]{1,0:T(8,128)(2,1)S(1)} %get-tuple-element.11, bf16[48,48]{1,0:T(8,128)(2,1)S(1)} %get-tuple-element.7, bf16[48,48]{1,0:T(8,128)(2,1)S(1)} %get-tuple-element.6), kind=kLoop, calls=%fused_computation | loop fusion | flops 165888 | bytes 46080 | tf_op jit(solution)/shard_map/concatenate | solution.py:481
  3.7 59.0 %slab_step.1 = (f32[8448,128]{1,0:T(8,128)}, f32[256,128]{1,0:T(8,128)}) custom-call(f32[8448,128]{1,0:T(8,128)} %bitcast.8, f32[256,128]{1,0:T(8,128)} %bitcast.11, f32[256,128]{1,0:T(8,128)} %bitcast.12, f32[1024,128]{1,0:T(8,128)} %bitcast.10, bf16[480,256]{1,0:T(8,128)(2,1)} %constant.7.clone.mats_h, f32[128,256]{1,0:T(8,128)} %constant.8.clone.tw_h, ...), custom_call_target="tpu_custom_call" | custom-call | tf_op jit(solution)/shard_map/slab_step/pallas_call | solution.py:485
  62.7 0.0 copy-start
  62.7 4.6 %copy.18 = f32[32,33,8,128]{3,2,1,0:T(8,128)} copy(f32[32,33,8,128]{3,2,1,0:T(8,128)} %bitcast.9) | data formatting | bytes 8650752
  67.3 0.0 copy-done
  67.3 0.7 copy.19
  (1 shorter events, 0.0 us)
Async XLA Ops:
  62.7 4.6 %copy-start = (f32[256,128]{1,0:T(8,128)S(1)}, f32[256,128]{1,0:T(8,128)}, u32[]{:S(2)}) copy-start(f32[256,128]{1,0:T(8,128)} %get-tuple-element.5) | copy-start | bytes 393220
where the time goes:
time: 68.1 us; the launch traced here: 67.9 us
  Pallas kernels  59 us (87%)
  local copies, waits for them, and re-layouts  6.89 us (10%)
  between operations  1.3 us (2%)
  other arithmetic  0.74 us (1%)
    pallas_call x1, Pallas kernels, body(): pl.pallas_call(kernel_body, out_shape=(jax.ShapeDtypeStruct((NL * LVL, 12...  59 us
    unnamed x6, local copies, waits for them, and re-layouts  6.89 us

commit v1 on v0

--- a/solution.py
+++ b/solution.py
@@ -60,15 +60,15 @@
 
 
 def kernel_body(
-    bins_h, u_h, w_h, binv_h, mats_h, tw_h, coll_h, ids_v, fall_s, cnt_s,
-    out_h, pres_h,
-    bins_v, out_v, u_v, w_v, binv_v, mats_v, tw_v, coll_v,
-    send1, x1, send2, x2, send3, x3, send4, ybuf,
+    bins_h, u_h, w_h, binv_h, mats_h, tw_h, kern_h, redi_h, ids_h, fall_h, cnt_h,
+    out_v, pres_v,
+    bins_v, u_v, w_v, binv_v, mats_v, tw_v, kern_v, redi_v, ids_v, fall_v, cnt_v, coll_v, fall_t,
+    send1, x1, send2, x2, send3, x3, send4, wtop,
     esend, edges, csend, corners, bpad, tpad,
-    whalo, zlo, zhi, send_f, send_l, send_u, halo_r, halo_l, halo_u, prior,
+    wlow, zlo, zhi, send_f, send_l, send_u, halo_r, halo_l, halo_u, prior,
     adv, fz, mask_v,
-    in_sem, bin_sem, out_sem, p_sem,
-    a2a_send, a2a_recv, e_send, e_recv, c_send, c_recv, h_send, h_recv,
+    in_sem, bin_sem,
+    a2a_send, a2a_recv, e_send, e_recv, c_send, c_recv, h_send, h_recv, w_send, w_recv,
 ):
     me = lax.axis_index("gx")
     g = lax.axis_index("gz")
@@ -82,21 +82,42 @@
 
     barrier = pltpu.get_barrier_semaphore()
 
-    def greet_x(o, _):
-        pl.semaphore_signal(barrier, inc=1, device_id={"gx": lax.rem(me + o, NP)}, device_id_type=MESH)
+    def peer_of(t):
+        half = (t + 1) // 2
+        odd = lax.rem(t, 2)
+        o = 16 + odd * half - (1 - odd) * half
+        return lax.rem(me + o, NP)
+
+    def greet(gx, gz):
+        pl.semaphore_signal(barrier, inc=1, device_id={"gx": gx, "gz": gz}, device_id_type=MESH)
+
+    def greet_x(t, _):
+        greet(peer_of(t), g)
         return 0
 
     def greet_z(o, _):
-        pl.semaphore_signal(barrier, inc=1, device_id={"gz": lax.rem(g + o, NG)}, device_id_type=MESH)
-        return 0
-
-    lax.fori_loop(1, NP, greet_x, 0)
+        greet(me, lax.rem(g + o, NG))
+        return 0
+
+    def greet_low(o, _):
+        greet(o, lax.rem(g + NG - 1, NG))
+        return 0
+
+    not_first = g > 0
+    not_last = g < NG - 1
+    takes_w = (me == 0) & not_first
+    lax.fori_loop(0, NP - 1, greet_x, 0)
     lax.fori_loop(1, NG, greet_z, 0)
+
+    @pl.when(takes_w)
+    def _():
+        lax.fori_loop(1, NP, greet_low, 0)
 
     loads = [
         pltpu.make_async_copy(s, d, in_sem.at[i])
         for i, (s, d) in enumerate(
-            [(u_h, u_v), (w_h, w_v), (binv_h, binv_v), (mats_h, mats_v), (tw_h, tw_v), (coll_h, coll_v)]
+            [(u_h, u_v), (w_h, w_v), (binv_h, binv_v), (mats_h, mats_v), (tw_h, tw_v),
+             (kern_h, kern_v), (redi_h, redi_v), (ids_h, ids_v), (fall_h, fall_v), (cnt_h, cnt_v)]
         )
     ]
     loads[0].start()
@@ -128,12 +149,21 @@
 
     lax.fori_loop(1, NL, div_step, 0)
 
-    pl.semaphore_wait(barrier, NP - 1 + NG - 1)
-
-    w_copy = pltpu.make_async_remote_copy(
-        src_ref=w_v.at[pl.ds(248, 8)], dst_ref=whalo, send_sem=h_send.at[0], recv_sem=h_recv.at[0],
-        device_id=above, device_id_type=MESH)
-    w_copy.start()
+    @pl.when(jnp.logical_not(takes_w))
+    def _():
+        wtop[...] = jnp.zeros((256, 128), F32)
+
+    extra = jnp.where(not_last & (me != 0), 1, 0)
+    pl.semaphore_wait(barrier, NP - 1 + NG - 1 + extra)
+
+    def w_msg(p):
+        return pltpu.make_async_remote_copy(
+            src_ref=w_v.at[pl.ds(248, 8)], dst_ref=wtop.at[pl.ds(pl.multiple_of(p * 8, 8), 8)],
+            send_sem=w_send, recv_sem=w_recv.at[p], device_id={"gx": me * 0, "gz": lax.rem(g + 1, NG)}, device_id_type=MESH)
+
+    @pl.when(not_last)
+    def _():
+        w_msg(me).start()
 
     def msg(stage, src, dst, rows, peer, at):
         s0 = pl.multiple_of(peer * at, 8)
@@ -143,21 +173,9 @@
             send_sem=a2a_send.at[stage, peer], recv_sem=a2a_recv.at[stage, me],
             device_id={"gx": peer}, device_id_type=MESH)
 
-    def peer_of(t):
-        half = (t + 1) // 2
-        odd = lax.rem(t, 2)
-        o = 16 + odd * half - (1 - odd) * half
-        return lax.rem(me + o, NP)
-
-    def send_all(stage, src, dst, rows, at, skip=False):
+    def send_all(stage, src, dst, rows, at):
         def step(t, _):
-            peer = peer_of(t)
-            if skip:
-                @pl.when(peer != 0)
-                def _():
-                    msg(stage, src, dst, rows, peer, at).start()
-            else:
-                msg(stage, src, dst, rows, peer, at).start()
+            msg(stage, src, dst, rows, peer_of(t), at).start()
             return 0
         lax.fori_loop(0, NP - 1, step, 0)
 
@@ -176,7 +194,8 @@
         m0 = pl.multiple_of(me * at, 8)
         dst[pl.ds(m0, rows), :] = src[pl.ds(m0, rows), :]
 
-    send_all(0, send1, x1, 9, 16, skip=True)
+    send_all(0, send1, x1, 9, 16)
+    own(send1, x1, 16, 16)
 
     bin_loads[7].wait()
     bin_loads[0].wait()
@@ -186,18 +205,12 @@
     z_down = pltpu.make_async_remote_copy(
         src_ref=bins_v.at[pl.ds(0, LVL)], dst_ref=zhi, send_sem=h_send.at[2], recv_sem=h_recv.at[2],
         device_id=below, device_id_type=MESH)
+    w_up = pltpu.make_async_remote_copy(
+        src_ref=w_v.at[pl.ds(248, 8)], dst_ref=wlow, send_sem=h_send.at[0], recv_sem=h_recv.at[0],
+        device_id=above, device_id_type=MESH)
+    w_up.start()
     z_up.start()
     z_down.start()
-
-    w_copy.wait()
-    not_first = g > 0
-    send1[pl.ds(0, 8), :] = send1[pl.ds(0, 8), :] - jnp.where(not_first, whalo[...], 0.0)
-
-    @pl.when(me != 0)
-    def _():
-        msg(0, send1, x1, 9, me * 0, 16).start()
-
-    own(send1, x1, 16, 16)
 
     loads[2].wait()
     csend[...] = jnp.zeros((8, 128), F32)
@@ -257,9 +270,12 @@
     for c in x_copies:
         c.start()
 
+    for c in loads[3:]:
+        c.wait()
+
     block = lax.broadcasted_iota(jnp.int32, (64, 64), 0)
     slot = lax.broadcasted_iota(jnp.int32, (64, 64), 1)
-    hits = (jnp.broadcast_to(ids_v[...], (64, 64)) == block) & (slot < cnt_s[0, 0])
+    hits = (jnp.broadcast_to(ids_v[...], (64, 64)) == block) & (slot < jnp.broadcast_to(cnt_v[...], (64, 64)))
     marks = jnp.max(jnp.where(hits, 1.0, 0.0), axis=1, keepdims=True)
     col_block = lax.broadcasted_iota(jnp.int32, (16, 128), 1) // 8
     row_block = lax.broadcasted_iota(jnp.int32, (16, 128), 0)
@@ -268,33 +284,16 @@
         mask_v[pl.ds(bz, 1), :] = jnp.sum(jnp.where(col_block == row_block, wide, 0.0), axis=0, keepdims=True)
 
     adv[...] = jnp.zeros((NBP * 8, 128), F32)
-    for c in loads[3:]:
-        c.wait()
-
-    z_up.wait()
-    z_down.wait()
-    for c in x_copies:
-        c.wait()
-
-    def prior_step(i, _):
-        s = pl.ds(i * 8, 8)
-        speed = halo_u[s, :]
-        prior[s, :] = jnp.maximum(speed, 0.0) * halo_l[s, :] + jnp.minimum(speed, 0.0) * send_f[s, :]
-        return 0
-
-    lax.fori_loop(0, NL // 2, prior_step, 0)
-
-    not_last = g < NG - 1
-    w_low = jnp.where(not_first, whalo[...], 0.0)
-
-    def low_face(m, _):
-        s = pl.ds(m * 8, 8)
-        c = w_low - fall_s[m]
-        fz[s, :] = jnp.maximum(c, 0.0) * jnp.where(not_first, zlo[s, :], 0.0) + jnp.minimum(c, 0.0) * bins_v[s, :]
-        bins_v[pl.ds(NL * LVL + m * 8, 8), :] = jnp.where(not_last, zhi[s, :], 0.0)
-        return 0
-
-    lax.fori_loop(0, NB, low_face, 0)
+    coll_v[...] = jnp.zeros((2 * NBP, 3 * NBP), F32)
+    pos = lax.broadcasted_iota(jnp.int32, (NB, 3 * NBP), 1)
+    row = lax.broadcasted_iota(jnp.int32, (NB, 3 * NBP), 0)
+    pick_hi = jnp.where((pos == row) | (pos == row + 2 * NBP), 1.0, 0.0).astype(BF16)
+    pick_lo = jnp.where(pos == row + NBP, 1.0, 0.0).astype(BF16)
+    for n, ref in enumerate((kern_v, redi_v)):
+        hi, lo = split(ref[...])
+        coll_v[pl.ds(n * NBP, NB), :] = dot_t(hi, pick_hi) + dot_t(lo, pick_lo)
+    for m in range(NB):
+        fall_t[pl.ds(m * 8, 8), :] = jnp.broadcast_to(fall_v[:, m:m + 1], (8, 128))
 
     def level(z, i, r):
         u = u_v[pl.ds(z * 8, 8), :]
@@ -310,14 +309,14 @@
             nxt = jnp.where(lane == 127, jnp.broadcast_to(hr[:, k:k + 1], (8, 128)), pltpu.roll(b, 127, 1))
             flux = u_pos * b + u_neg * nxt
             prev = jnp.where(lane == 0, jnp.broadcast_to(pf[:, k:k + 1], (8, 128)), pltpu.roll(flux, 1, 1))
-            c = w - fall_s[m]
+            c = w - fall_t[pl.ds(m * 8, 8), :]
             top = jnp.maximum(c, 0.0) * b + jnp.minimum(c, 0.0) * up
             s = pl.ds(m * 8, 8)
             adv[s, :] = b - (flux - prev) - (top - fz[s, :])
             fz[s, :] = top
         mark = jnp.broadcast_to(mask_v[pl.ds(z // 8, 1), :], (NBP, 128))
-        grow_w = coll_v[pl.ds(0, NBP), :]
-        redi_w = coll_v[pl.ds(NBP, NBP), :]
+        grow_w = coll_v[pl.ds(0, NBP), :].astype(BF16)
+        redi_w = coll_v[pl.ds(NBP, NBP), :].astype(BF16)
         for h in range(4):
             ys = (2 * h, 2 * h + 1)
             v = jnp.concatenate([adv[pl.ds(y, NBP, stride=8), :] for y in ys], axis=1)
@@ -330,21 +329,22 @@
                 new = v[:, part] + tend[:, part] * mark
                 out_v[pl.ds(base + y, NB, stride=8), :] = new[:NB]
 
-    def flush(z2):
-        s = pl.ds(z2 * 2 * LVL, 2 * LVL)
-        return pltpu.make_async_copy(out_v.at[s], out_h.at[s], out_sem.at[z2])
-
     def levels(first, last):
         def step(i, _):
             level(2 * i, i, 0)
             level(2 * i + 1, i, 1)
-            flush(i).start()
             return 0
         lax.fori_loop(first, last, step, 0)
 
-    levels(0, CUT[0])
-
     wait_all(0, send1, x1, 9, 16)
+
+    @pl.when(takes_w)
+    def _():
+        def step(p, _):
+            w_msg(p).wait_recv()
+            return 0
+        lax.fori_loop(0, NP, step, 0)
+
     borders = x1[pl.ds(8, NP, stride=16), :]
     borders = pltpu.roll(borders, 1, 0)
     lane32 = lax.broadcasted_iota(jnp.int32, (32, 128), 1)
@@ -355,7 +355,7 @@
     for h in range(4):
         us = []
         for y in (2 * h, 2 * h + 1):
-            xy = x1[pl.ds(y, NP, stride=16), :]
+            xy = x1[pl.ds(y, NP, stride=16), :] - wtop[pl.ds(y, NP, stride=8), :]
             shifted = borders if y == 0 else pltpu.roll(borders, 128 - y, 1)
             xy = xy - jnp.where(lane32 == 0, shifted, 0.0)
             hi, lo = split(xy)
@@ -372,7 +372,33 @@
     send_all(1, send2, x2, 16, 16)
     own(send2, x2, 16, 16)
 
-    levels(CUT[0], CUT[1])
+    z_up.wait()
+    w_up.wait()
+    z_down.wait()
+    for c in x_copies:
+        c.wait()
+
+    def prior_step(i, _):
+        s = pl.ds(i * 8, 8)
+        speed = halo_u[s, :]
+        prior[s, :] = jnp.maximum(speed, 0.0) * halo_l[s, :] + jnp.minimum(speed, 0.0) * send_f[s, :]
+        return 0
+
+    lax.fori_loop(0, NL // 2, prior_step, 0)
+
+    w_low = jnp.where(not_first, wlow[...], 0.0)
+
+    def low_face(m, _):
+        s = pl.ds(m * 8, 8)
+        c = w_low - fall_t[s, :]
+        fz[s, :] = jnp.maximum(c, 0.0) * jnp.where(not_first, zlo[s, :], 0.0) + jnp.minimum(c, 0.0) * bins_v[s, :]
+        bins_v[pl.ds(NL * LVL + m * 8, 8), :] = jnp.where(not_last, zhi[s, :], 0.0)
+        return 0
+
+    lax.fori_loop(0, NB, low_face, 0)
+
+
+    levels(0, CUT[0])
 
     wait_all(1, send2, x2, 16, 16)
 
@@ -397,6 +423,7 @@
         return 0
 
     lax.fori_loop(0, NL // 4, solve_step, 0)
+    levels(CUT[0], CUT[1])
     wait_z(csend, corners, 8, c_send, c_recv)
     wait_z(esend, edges, 32, e_send, e_recv)
 
@@ -453,56 +480,66 @@
         pr = both[:32] + both[32:] + dot(h2[:32], lo)
         for n, y in enumerate((2 * h, 2 * h + 1)):
             send4[pl.ds(y, NP, stride=8), :] = pr[:, 128 * n:128 * n + 128]
-    send_all(3, send4, pres_h, 8, 8)
-    m0 = pl.multiple_of(me * 8, 8)
-    own_copy = pltpu.make_async_copy(send4.at[pl.ds(m0, 8)], pres_h.at[pl.ds(m0, 8)], p_sem)
-    own_copy.start()
+    send_all(3, send4, pres_v, 8, 8)
+    own(send4, pres_v, 8, 8)
 
     levels(CUT[2], NL // 2)
-    own_copy.wait()
-
-    def drain(i, _):
-        flush(i).wait()
-        return 0
-
-    lax.fori_loop(0, NL // 2, drain, 0)
-    wait_all(3, send4, pres_h, 8, 8)
-
-
-CUT = (4, 10, 16)
+
+    @pl.when(not_last)
+    def _():
+        w_msg(me).wait_send()
+
+    wait_all(3, send4, pres_v, 8, 8)
+
+
+def write_body(out_v, pres_v, out_h, pres_h, sem):
+    copies = [pltpu.make_async_copy(pres_v, pres_h, sem.at[8])]
+    for i in range(8):
+        s = pl.ds(i * 4 * LVL, 4 * LVL)
+        copies.append(pltpu.make_async_copy(out_v.at[s], out_h.at[s], sem.at[i]))
+    for c in copies:
+        c.start()
+    for c in copies:
+        c.wait()
+
+
+CUT = (6, 8, 14)
 
 
 def body(bins, u, w, fall, kern, redi, ids, counts, binv):
-    def stacked(m):
-        m = jnp.pad(m.T, ((0, NBP - NB), (0, NBP - NB)))
-        hi = lax.reduce_precision(m, 8, 7)
-        return jnp.concatenate([hi, m - hi, hi], axis=1)
-
-    coll = jnp.concatenate([stacked(kern), stacked(redi)], axis=0).astype(BF16)
     mats, tw = tables()
     vmem = lambda rows, cols=128, t=F32: pltpu.VMEM((rows, cols), t)
     dma = pltpu.SemaphoreType.DMA
     out, pres = pl.pallas_call(
         kernel_body,
-        out_shape=(jax.ShapeDtypeStruct((NL * LVL, 128), F32), jax.ShapeDtypeStruct((NL * 8, 128), F32)),
-        in_specs=[pl.BlockSpec(memory_space=pl.ANY)] * 7
-        + [pl.BlockSpec(memory_space=pltpu.VMEM), pl.BlockSpec(memory_space=pltpu.SMEM), pl.BlockSpec(memory_space=pltpu.SMEM)],
-        out_specs=[pl.BlockSpec(memory_space=pl.ANY)] * 2,
+        out_shape=(pltpu.VMEM((NL * LVL, 128), F32), pltpu.VMEM((NL * 8, 128), F32)),
+        in_specs=[pl.BlockSpec(memory_space=pl.ANY)] * 11,
+        out_specs=[pl.BlockSpec(memory_space=pltpu.VMEM)] * 2,
         scratch_shapes=[
-            vmem((NL + 1) * LVL), vmem(NL * LVL), vmem(256), vmem(256), vmem(1024), vmem(480, 256, BF16), vmem(128, 256), vmem(2 * NBP, 3 * NBP, BF16),
-            vmem(512), vmem(512), vmem(512), vmem(512), vmem(512), vmem(512), vmem(256), vmem(8),
+            vmem((NL + 1) * LVL), vmem(256), vmem(256), vmem(1024), vmem(480, 256, BF16), vmem(128, 256),
+            vmem(NB, NB), vmem(NB, NB), vmem(1, 64, jnp.int32), vmem(1, NB), vmem(1, 1, jnp.int32), vmem(2 * NBP, 3 * NBP), vmem(LVL),
+            vmem(512), vmem(512), vmem(512), vmem(512), vmem(512), vmem(512), vmem(256), vmem(256),
             vmem(32), vmem(NG * 32), vmem(8), vmem(NG * 8), vmem((NG + 1) * 16), vmem((NG + 1) * 16),
             vmem(8), vmem(LVL), vmem(LVL), vmem(128), vmem(128), vmem(128), vmem(128), vmem(128), vmem(128), vmem(128),
             vmem(NBP * 8), vmem(LVL), vmem(8),
-            dma((6,)), dma((8,)), dma((16,)), dma,
-            dma((4, NP)), dma((4, NP)), dma((NG,)), dma((NG,)), dma((NG,)), dma((NG,)), dma((6,)), dma((6,)),
+            dma((10,)), dma((8,)),
+            dma((4, NP)), dma((4, NP)), dma((NG,)), dma((NG,)), dma((NG,)), dma((NG,)), dma((6,)), dma((6,)), dma, dma((NP,)),
         ],
-        compiler_params=pltpu.CompilerParams(collective_id=0, has_side_effects=True, vmem_limit_bytes=60 * 1024 * 1024),
+        compiler_params=pltpu.CompilerParams(collective_id=0, has_side_effects=True, vmem_limit_bytes=24 * 1024 * 1024),
         name="slab_step",
     )(
         bins.reshape(NL * LVL, 128), u.reshape(256, 128), w.reshape(256, 128), binv.reshape(1024, 128),
-        jnp.asarray(mats), jnp.asarray(tw), coll, ids, fall, counts,
+        jnp.asarray(mats), jnp.asarray(tw), kern, redi, ids, fall.reshape(1, NB), counts,
     )
+    out, pres = pl.pallas_call(
+        write_body,
+        out_shape=(jax.ShapeDtypeStruct((NL * LVL, 128), F32), jax.ShapeDtypeStruct((NL * 8, 128), F32)),
+        in_specs=[pl.BlockSpec(memory_space=pltpu.VMEM)] * 2,
+        out_specs=[pl.BlockSpec(memory_space=pl.ANY)] * 2,
+        scratch_shapes=[dma((9,))],
+        compiler_params=pltpu.CompilerParams(vmem_limit_bytes=1024 * 1024),
+        name="write_out",
+    )(out, pres)
     return out.reshape(NL, NB, 8, 128), pres.reshape(NL, 8, 128)
 
 

time: 68.1 us -> 66.2 us (0.972)
  Pallas kernels: 59 us -> 54.9 us
  local copies, waits for them, and re-layouts: 6.89 us -> 9.68 us
  other arithmetic: 0.74 us -> 0 us
    pallas_call x1 -> x2, Pallas kernels: 59 us -> 54.9 us  [the longest x1 52.7 us: body(): pl.pallas_call(kernel_body, out_shape=(pltpu.VMEM((NL * LVL, 128), F32),...]
    unnamed x6 -> x20, local copies, waits for them, and re-layouts: 6.89 us -> 9.68 us
    concatenate x1 -> x0, other arithmetic: 0.72 us -> none  [body(): coll = jnp.concatenate([stacked(kern), stacked(redi)], axis=0).astype(BF16)]
where the time goes in v1:
time: 66.2 us; the launch traced here: 65.8 us
  Pallas kernels  54.9 us (83%)
  local copies, waits for them, and re-layouts  9.68 us (15%)
  between operations  1.3 us (2%)
    pallas_call x1, Pallas kernels, body(): pl.pallas_call(kernel_body, out_shape=(pltpu.VMEM((NL * LVL, 128), F32),...  52.7 us
    unnamed x20, local copies, waits for them, and re-layouts  9.68 us
    pallas_call x1, Pallas kernels, body(): pl.pallas_call(write_body, out_shape=(jax.ShapeDtypeStruct((NL * LVL, 128...  2.16 us

profile of v1, /device:TPU:1, one launch (start us, length us, event | category | flops | bytes accessed | tf_op | source)
XLA Modules:
  0.0 65.8 jit_solution(13355978489218069793)
XLA Ops:
  1.3 0.0 copy-start
  1.3 2.2 %copy-done = f32[32,33,8,128]{3,2,1,0:T(8,128)S(1)} copy-done((f32[32,33,8,128]{3,2,1,0:T(8,128)S(1)}, f32[32,33,8,128]{3,2,1,0:T(8,128)}, u32[]{:S(2)}) %copy-start) | copy-done | bytes 4325400
  3.5 0.0 copy-start.1
  3.5 1.0 %copy-done.1 = f32[32,32,128]{2,1,0:T(8,128)S(1)} copy-done((f32[32,32,128]{2,1,0:T(8,128)S(1)}, f32[32,32,128]{2,1,0:T(8,128)}, u32[]{:S(2)}) %copy-start.1) | copy-done | bytes 524312
  4.5 0.0 copy-start.2
  4.5 0.9 %copy-done.2 = bf16[480,256]{1,0:T(8,128)(2,1)S(1)} copy-done((bf16[480,256]{1,0:T(8,128)(2,1)S(1)}, bf16[480,256]{1,0:T(8,128)(2,1)}, u32[]{:S(2)}) %copy-start.2) | copy-done | bytes 245784
  5.5 0.0 copy-start.3
  5.5 0.9 %copy-done.3 = f32[32,8,128]{2,1,0:T(8,128)S(1)} copy-done((f32[32,8,128]{2,1,0:T(8,128)S(1)}, f32[32,8,128]{2,1,0:T(8,128)}, u32[]{:S(2)}) %copy-start.3) | copy-done | bytes 131096
  6.4 0.0 copy-start.4
  6.4 0.9 %copy-done.4 = f32[32,8,128]{2,1,0:T(8,128)S(1)} copy-done((f32[32,8,128]{2,1,0:T(8,128)S(1)}, f32[32,8,128]{2,1,0:T(8,128)}, u32[]{:S(2)}) %copy-start.4) | copy-done | bytes 131096
  7.3 0.0 copy-start.5
  7.3 0.9 %copy-done.5 = f32[128,256]{1,0:T(8,128)S(1)} copy-done((f32[128,256]{1,0:T(8,128)S(1)}, f32[128,256]{1,0:T(8,128)}, u32[]{:S(2)}) %copy-start.5) | copy-done | bytes 131096
  8.2 0.0 copy-start.6
  8.2 0.7 %copy-done.6 = f32[33,33]{1,0:T(8,128)S(1)} copy-done((f32[33,33]{1,0:T(8,128)S(1)}, f32[33,33]{1,0:T(8,128)}, u32[]{:S(2)}) %copy-start.6) | copy-done | bytes 4380
  8.9 0.0 copy-start.7
  8.9 0.7 %copy-done.7 = f32[33,33]{1,0:T(8,128)S(1)} copy-done((f32[33,33]{1,0:T(8,128)S(1)}, f32[33,33]{1,0:T(8,128)}, u32[]{:S(2)}) %copy-start.7) | copy-done | bytes 4380
  9.7 0.0 copy-start.8
  9.7 0.7 copy-done.8
  10.3 0.0 copy-start.9
  10.3 0.7 copy-done.9
  11.0 52.7 %slab_step.1 = (f32[8448,128]{1,0:T(8,128)S(1)}, f32[256,128]{1,0:T(8,128)S(1)}) custom-call(f32[8448,128]{1,0:T(8,128)S(1)} %bitcast.7, f32[256,128]{1,0:T(8,128)S(1)} %bitcast.9, f32[256,128]{1,0:T(8,128)S(1)} %bitcast.10, f32[1024,128]{1,0:T(8,128)S(1)} %bitcast.8, bf16[480,256]{1,0:T(8,128)(2,1)S(1)} %copy-done.2, f32[128,256]{1,0:T(8,128)S(1)} %copy-done.5, ...), custom_call_target="tpu_custom_call" | custom-call | tf_op jit(solution)/shard_map/slab_step/pallas_call | solution.py:513
  63.7 2.2 %write_out.1 = (f32[8448,128]{1,0:T(8,128)}, f32[256,128]{1,0:T(8,128)}) custom-call(f32[8448,128]{1,0:T(8,128)S(1)} %get-tuple-element.6.out_v, f32[256,128]{1,0:T(8,128)S(1)} %get-tuple-element.7.pres_v), custom_call_target="tpu_custom_call" | custom-call | tf_op jit(solution)/shard_map/write_out/pallas_call | solution.py:534
Async XLA Ops:
  1.3 2.2 %copy-start = (f32[32,33,8,128]{3,2,1,0:T(8,128)S(1)}, f32[32,33,8,128]{3,2,1,0:T(8,128)}, u32[]{:S(2)}) copy-start(f32[32,33,8,128]{3,2,1,0:T(8,128)} %param.11) | copy-start | bytes 12976132
  3.5 1.0 %copy-start.1 = (f32[32,32,128]{2,1,0:T(8,128)S(1)}, f32[32,32,128]{2,1,0:T(8,128)}, u32[]{:S(2)}) copy-start(f32[32,32,128]{2,1,0:T(8,128)} %param.19) | copy-start | bytes 1572868
  4.5 0.9 %copy-start.2 = (bf16[480,256]{1,0:T(8,128)(2,1)S(1)}, bf16[480,256]{1,0:T(8,128)(2,1)}, u32[]{:S(2)}) copy-start(bf16[480,256]{1,0:T(8,128)(2,1)} %constant.4.clone.mats_h) | copy-start | bytes 737284
  5.5 0.9 %copy-start.3 = (f32[32,8,128]{2,1,0:T(8,128)S(1)}, f32[32,8,128]{2,1,0:T(8,128)}, u32[]{:S(2)}) copy-start(f32[32,8,128]{2,1,0:T(8,128)} %param.12) | copy-start | bytes 393220
  6.4 0.9 %copy-start.4 = (f32[32,8,128]{2,1,0:T(8,128)S(1)}, f32[32,8,128]{2,1,0:T(8,128)}, u32[]{:S(2)}) copy-start(f32[32,8,128]{2,1,0:T(8,128)} %param.13) | copy-start | bytes 393220
  7.3 0.9 %copy-start.5 = (f32[128,256]{1,0:T(8,128)S(1)}, f32[128,256]{1,0:T(8,128)}, u32[]{:S(2)}) copy-start(f32[128,256]{1,0:T(8,128)} %constant.5.clone.tw_h) | copy-start | bytes 393220
  8.2 0.7 %copy-start.6 = (f32[33,33]{1,0:T(8,128)S(1)}, f32[33,33]{1,0:T(8,128)}, u32[]{:S(2)}) copy-start(f32[33,33]{1,0:T(8,128)} %kern_h.1) | copy-start | bytes 13072
  8.9 0.7 %copy-start.7 = (f32[33,33]{1,0:T(8,128)S(1)}, f32[33,33]{1,0:T(8,128)}, u32[]{:S(2)}) copy-start(f32[33,33]{1,0:T(8,128)} %redi_h.1) | copy-start | bytes 13072
  9.7 0.7 copy-start.8
  10.3 0.7 copy-start.9

commit v2 on v1

--- a/solution.py
+++ b/solution.py
@@ -513,7 +513,7 @@
     out, pres = pl.pallas_call(
         kernel_body,
         out_shape=(pltpu.VMEM((NL * LVL, 128), F32), pltpu.VMEM((NL * 8, 128), F32)),
-        in_specs=[pl.BlockSpec(memory_space=pl.ANY)] * 11,
+        in_specs=[pl.BlockSpec(memory_space=pltpu.HBM)] * 11,
         out_specs=[pl.BlockSpec(memory_space=pltpu.VMEM)] * 2,
         scratch_shapes=[
             vmem((NL + 1) * LVL), vmem(256), vmem(256), vmem(1024), vmem(480, 256, BF16), vmem(128, 256),
@@ -525,7 +525,7 @@
             dma((10,)), dma((8,)),
             dma((4, NP)), dma((4, NP)), dma((NG,)), dma((NG,)), dma((NG,)), dma((NG,)), dma((6,)), dma((6,)), dma, dma((NP,)),
         ],
-        compiler_params=pltpu.CompilerParams(collective_id=0, has_side_effects=True, vmem_limit_bytes=24 * 1024 * 1024),
+        compiler_params=pltpu.CompilerParams(collective_id=0, has_side_effects=True, vmem_limit_bytes=62300000),
         name="slab_step",
     )(
         bins.reshape(NL * LVL, 128), u.reshape(256, 128), w.reshape(256, 128), binv.reshape(1024, 128),

time: 66.2 us -> 56.5 us (0.85)
  local copies, waits for them, and re-layouts: 9.68 us -> 0 us
    unnamed x20 -> x0, local copies, waits for them, and re-layouts: 9.68 us -> none
where the time goes in v2:
time: 56.5 us; the launch traced here: 56.4 us
  Pallas kernels  55.1 us (98%)
  between operations  1.29 us (2%)
    pallas_call x1, Pallas kernels, body(): pl.pallas_call(kernel_body, out_shape=(pltpu.VMEM((NL * LVL, 128), F32),...  53 us
    pallas_call x1, Pallas kernels, body(): pl.pallas_call(write_body, out_shape=(jax.ShapeDtypeStruct((NL * LVL, 128...  2.16 us

profile of v2, /device:TPU:1, one launch (start us, length us, event | category | flops | bytes accessed | tf_op | source)
XLA Modules:
  0.0 56.4 jit_solution(4063543715053183563)
XLA Ops:
  1.3 53.0 %slab_step.1 = (f32[8448,128]{1,0:T(8,128)S(1)}, f32[256,128]{1,0:T(8,128)S(1)}) custom-call(f32[8448,128]{1,0:T(8,128)} %bitcast.7, f32[256,128]{1,0:T(8,128)} %bitcast.9, f32[256,128]{1,0:T(8,128)} %bitcast.10, f32[1024,128]{1,0:T(8,128)} %bitcast.8, bf16[480,256]{1,0:T(8,128)(2,1)} %constant.4.clone.mats_h, f32[128,256]{1,0:T(8,128)} %constant.5.clone.tw_h, ...), custom_call_target="tpu_custom_call" | custom-call | tf_op jit(solution)/shard_map/slab_step/pallas_call | solution.py:513
  54.3 2.2 %write_out.1 = (f32[8448,128]{1,0:T(8,128)}, f32[256,128]{1,0:T(8,128)}) custom-call(f32[8448,128]{1,0:T(8,128)S(1)} %get-tuple-element.6.out_v, f32[256,128]{1,0:T(8,128)S(1)} %get-tuple-element.7.pres_v), custom_call_target="tpu_custom_call" | custom-call | tf_op jit(solution)/shard_map/write_out/pallas_call | solution.py:534

commit v3 on v2

--- a/solution.py
+++ b/solution.py
@@ -64,8 +64,8 @@
     out_v, pres_v,
     bins_v, u_v, w_v, binv_v, mats_v, tw_v, kern_v, redi_v, ids_v, fall_v, cnt_v, coll_v, fall_t,
     send1, x1, send2, x2, send3, x3, send4, wtop,
-    esend, edges, csend, corners, bpad, tpad,
-    wlow, zlo, zhi, send_f, send_l, send_u, halo_r, halo_l, halo_u, prior,
+    esend, edges, csend, corners,
+    wlow, zlo, zhi, send_f, send_l, halo_r, halo_l, prior,
     adv, fz, mask_v,
     in_sem, bin_sem,
     a2a_send, a2a_recv, e_send, e_recv, c_send, c_recv, h_send, h_recv, w_send, w_recv,
@@ -91,14 +91,6 @@
     def greet(gx, gz):
         pl.semaphore_signal(barrier, inc=1, device_id={"gx": gx, "gz": gz}, device_id_type=MESH)
 
-    def greet_x(t, _):
-        greet(peer_of(t), g)
-        return 0
-
-    def greet_z(o, _):
-        greet(me, lax.rem(g + o, NG))
-        return 0
-
     def greet_low(o, _):
         greet(o, lax.rem(g + NG - 1, NG))
         return 0
@@ -106,12 +98,7 @@
     not_first = g > 0
     not_last = g < NG - 1
     takes_w = (me == 0) & not_first
-    lax.fori_loop(0, NP - 1, greet_x, 0)
-    lax.fori_loop(1, NG, greet_z, 0)
-
-    @pl.when(takes_w)
-    def _():
-        lax.fori_loop(1, NP, greet_low, 0)
+    near = [(d, (g + d >= 0) & (g + d < NG)) for d in (3, -3, 2, -2, 1, -1)]
 
     loads = [
         pltpu.make_async_copy(s, d, in_sem.at[i])
@@ -122,6 +109,18 @@
     ]
     loads[0].start()
     loads[1].start()
+    for t in range(NP - 1):
+        half = (t + 1) // 2
+        greet(lax.rem(me + (16 + half if t % 2 else 16 - half), NP), g)
+    for d, there in near:
+        @pl.when(there)
+        def _(d=d):
+            greet(me, g + d)
+
+    @pl.when(takes_w)
+    def _():
+        lax.fori_loop(1, NP, greet_low, 0)
+
     bin_loads = [
         pltpu.make_async_copy(bins_h.at[pl.ds(i * 4 * LVL, 4 * LVL)], bins_v.at[pl.ds(i * 4 * LVL, 4 * LVL)], bin_sem.at[i])
         for i in range(8)
@@ -142,19 +141,16 @@
         send1[pl.ds(q * 16 + 8, 8), :] = jnp.broadcast_to(row, (8, 128))
 
     tile_div(0, jnp.zeros((8, 128), F32))
-
-    def div_step(q, _):
+    for q in range(1, NL):
         tile_div(q, w_v[pl.ds(q * 8 - 8, 8), :])
-        return 0
-
-    lax.fori_loop(1, NL, div_step, 0)
 
     @pl.when(jnp.logical_not(takes_w))
     def _():
         wtop[...] = jnp.zeros((256, 128), F32)
 
     extra = jnp.where(not_last & (me != 0), 1, 0)
-    pl.semaphore_wait(barrier, NP - 1 + NG - 1 + extra)
+    n_near = jnp.minimum(g, 3) + jnp.minimum(NG - 1 - g, 3)
+    pl.semaphore_wait(barrier, NP - 1 + n_near + extra)
 
     def w_msg(p):
         return pltpu.make_async_remote_copy(
@@ -208,64 +204,84 @@
     w_up = pltpu.make_async_remote_copy(
         src_ref=w_v.at[pl.ds(248, 8)], dst_ref=wlow, send_sem=h_send.at[0], recv_sem=h_recv.at[0],
         device_id=above, device_id_type=MESH)
-    w_up.start()
-    z_up.start()
-    z_down.start()
+
+    @pl.when(not_last)
+    def _():
+        w_up.start()
+        z_up.start()
+
+    @pl.when(not_first)
+    def _():
+        z_down.start()
+
+    @pl.when(jnp.logical_not(not_first))
+    def _():
+        wlow[...] = jnp.zeros((8, 128), F32)
+        zlo[...] = jnp.zeros((LVL, 128), F32)
+
+    @pl.when(jnp.logical_not(not_last))
+    def _():
+        zhi[...] = jnp.zeros((LVL, 128), F32)
 
     loads[2].wait()
     csend[...] = jnp.zeros((8, 128), F32)
     for i, r in enumerate((0, 31, 31 * 32, 31 * 32 + 31)):
         csend[pl.ds(i, 1), :] = binv_v[pl.ds(r, 1), :]
 
-    def z_msg(src, dst, rows, peer, ss, rs):
-        d0 = pl.multiple_of(g * rows, 8)
+    def corner_msg(d, group):
         return pltpu.make_async_remote_copy(
-            src_ref=src, dst_ref=dst.at[pl.ds(d0, rows)], send_sem=ss.at[peer], recv_sem=rs.at[g],
-            device_id={"gz": peer}, device_id_type=MESH)
-
-    def send_z(src, dst, rows, ss, rs):
-        def step(o, _):
-            z_msg(src, dst, rows, lax.rem(g + o, NG), ss, rs).start()
-            return 0
-        lax.fori_loop(1, NG, step, 0)
-        dst[pl.ds(pl.multiple_of(g * rows, 8), rows), :] = src[...]
-
-    def wait_z(src, dst, rows, ss, rs):
-        def step(o, _):
-            peer = lax.rem(g + o, NG)
-            pltpu.make_async_remote_copy(
-                src_ref=src, dst_ref=dst.at[pl.ds(pl.multiple_of(peer * rows, 8), rows)], send_sem=ss.at[peer], recv_sem=rs.at[peer],
-                device_id={"gz": peer}, device_id_type=MESH).wait()
-            return 0
-        lax.fori_loop(1, NG, step, 0)
-
-    send_z(csend, corners, 8, c_send, c_recv)
+            src_ref=csend, dst_ref=corners.at[pl.ds(pl.multiple_of((group + 3) * 8, 8), 8)],
+            send_sem=c_send.at[d + 3], recv_sem=c_recv.at[group], device_id={"gz": lax.rem(g + d + NG, NG)}, device_id_type=MESH)
+
+    def edge_msg(d, group, toward):
+        first = 16 if abs(d) > 1 and toward > 0 else 0
+        rows = 32 if abs(d) == 1 else 16
+        return pltpu.make_async_remote_copy(
+            src_ref=esend.at[pl.ds(first, rows)], dst_ref=edges.at[pl.ds(pl.multiple_of((group + 3) * 32 + first, 8), rows)],
+            send_sem=e_send.at[d + 3], recv_sem=e_recv.at[group], device_id={"gz": lax.rem(g + d + NG, NG)}, device_id_type=MESH)
+
+    for lo in (0, NG + 3):
+        edges[pl.ds(lo * 32, 96), :] = jnp.zeros((96, 128), F32)
+        corners[pl.ds(lo * 8, 24), :] = jnp.zeros((24, 128), F32)
+    corners[pl.ds(pl.multiple_of((g + 3) * 8, 8), 8), :] = csend[...]
+    for d, there in near:
+        @pl.when(there)
+        def _(d=d):
+            corner_msg(d, g).start()
 
     for i in range(1, 7):
         bin_loads[i].wait()
 
+    turned = lax.rem(lane + 1, 128)
+
+    def columns(vs):
+        items = [(v, 1) for v in vs]
+        while len(items) > 1:
+            merged = []
+            for n in range(0, len(items) - 1, 2):
+                (a, ca), (b, cb) = items[n], items[n + 1]
+                merged.append((jnp.where(turned < 2 * ca, a, pltpu.roll(b, 2 * ca, 1)), ca + cb))
+            if len(items) % 2:
+                merged.append(items[-1])
+            items = merged
+        return items[0][0]
+
+    even = lax.rem(lane, 2) == 0
+
     def pack(i, _):
-        first = jnp.zeros((8, 128), F32)
-        last = jnp.zeros((8, 128), F32)
+        sides = []
         for r in range(2):
-            for m in range(NB):
-                v = bins_v[pl.ds((2 * i + r) * LVL + m * 8, 8), :]
-                hit = lane == (NB * r + m)
-                first = jnp.where(hit, jnp.broadcast_to(v[:, 0:1], (8, 128)), first)
-                last = jnp.where(hit, jnp.broadcast_to(v[:, 127:128], (8, 128)), last)
-        speeds = jnp.where(
-            lane < NB,
-            jnp.broadcast_to(u_v[pl.ds(i * 16, 8), :][:, 127:128], (8, 128)),
-            jnp.broadcast_to(u_v[pl.ds(i * 16 + 8, 8), :][:, 127:128], (8, 128)))
-        send_f[pl.ds(i * 8, 8), :] = first
-        send_l[pl.ds(i * 8, 8), :] = last
-        send_u[pl.ds(i * 8, 8), :] = speeds
+            tiles = [bins_v[pl.ds((2 * i + r) * LVL + m * 8, 8), :] for m in range(NB)]
+            sides.append(columns(tiles + [u_v[pl.ds((2 * i + r) * 8, 8), :]]))
+        other = pltpu.roll(sides[1], 1, 1)
+        send_f[pl.ds(i * 8, 8), :] = jnp.where(even, sides[0], other)
+        send_l[pl.ds(i * 8, 8), :] = jnp.where(even, other, sides[0])
         return 0
 
     lax.fori_loop(0, NL // 2, pack, 0)
     x_copies = [
         pltpu.make_async_remote_copy(src_ref=s, dst_ref=d, send_sem=h_send.at[i], recv_sem=h_recv.at[i], device_id=to, device_id_type=MESH)
-        for i, s, d, to in ((3, send_f, halo_r, left), (4, send_l, halo_l, right), (5, send_u, halo_u, right))
+        for i, s, d, to in ((3, send_f, halo_r, left), (4, send_l, halo_l, right))
     ]
     for c in x_copies:
         c.start()
@@ -303,12 +319,13 @@
         pf = prior[pl.ds(i * 8, 8), :]
         base = z * LVL
         for m in range(NB):
-            k = NB * r + m
+            k = 2 * m + r
+            kl = (k + 127) % 128
             b = bins_v[pl.ds(base + m * 8, 8), :]
             up = bins_v[pl.ds(base + LVL + m * 8, 8), :]
             nxt = jnp.where(lane == 127, jnp.broadcast_to(hr[:, k:k + 1], (8, 128)), pltpu.roll(b, 127, 1))
             flux = u_pos * b + u_neg * nxt
-            prev = jnp.where(lane == 0, jnp.broadcast_to(pf[:, k:k + 1], (8, 128)), pltpu.roll(flux, 1, 1))
+            prev = jnp.where(lane == 0, jnp.broadcast_to(pf[:, kl:kl + 1], (8, 128)), pltpu.roll(flux, 1, 1))
             c = w - fall_t[pl.ds(m * 8, 8), :]
             top = jnp.maximum(c, 0.0) * b + jnp.minimum(c, 0.0) * up
             s = pl.ds(m * 8, 8)
@@ -372,16 +389,26 @@
     send_all(1, send2, x2, 16, 16)
     own(send2, x2, 16, 16)
 
-    z_up.wait()
-    w_up.wait()
-    z_down.wait()
+    @pl.when(not_last)
+    def _():
+        z_up.wait_send()
+        w_up.wait_send()
+        z_down.wait_recv()
+
+    @pl.when(not_first)
+    def _():
+        z_up.wait_recv()
+        w_up.wait_recv()
+        z_down.wait_send()
+
     for c in x_copies:
         c.wait()
 
     def prior_step(i, _):
         s = pl.ds(i * 8, 8)
-        speed = halo_u[s, :]
-        prior[s, :] = jnp.maximum(speed, 0.0) * halo_l[s, :] + jnp.minimum(speed, 0.0) * send_f[s, :]
+        edge = halo_l[s, :]
+        speed = jnp.where(even, jnp.broadcast_to(edge[:, 66:67], (8, 128)), jnp.broadcast_to(edge[:, 65:66], (8, 128)))
+        prior[s, :] = jnp.maximum(speed, 0.0) * edge + jnp.minimum(speed, 0.0) * pltpu.roll(send_f[s, :], 127, 1)
         return 0
 
     lax.fori_loop(0, NL // 2, prior_step, 0)
@@ -414,7 +441,11 @@
     low, high = apply_rows((0, 31))
     esend[pl.ds(0, 16), :] = low
     esend[pl.ds(16, 16), :] = high
-    send_z(esend, edges, 32, e_send, e_recv)
+    edges[pl.ds(pl.multiple_of((g + 3) * 32, 8), 32), :] = esend[...]
+    for d, there in near:
+        @pl.when(there)
+        def _(d=d):
+            edge_msg(d, g, d).start()
 
     def solve_step(t, _):
         rows = [t * 4 + n for n in range(4)]
@@ -424,32 +455,31 @@
 
     lax.fori_loop(0, NL // 4, solve_step, 0)
     levels(CUT[0], CUT[1])
-    wait_z(csend, corners, 8, c_send, c_recv)
-    wait_z(esend, edges, 32, e_send, e_recv)
-
-    zero = jnp.zeros((16, 128), F32)
-    e0 = [edges[pl.ds(k * 32, 16), :] for k in range(NG)]
-    e1 = [edges[pl.ds(k * 32 + 16, 16), :] for k in range(NG)]
-
-    def corner(k, i):
-        return jnp.broadcast_to(corners[pl.ds(k * 8 + i, 1), :], (16, 128))
-
-    bs, ts = e0, e1
-    for _ in range(2):
-        nb, nt = [], []
-        for k in range(NG):
-            over = bs[k + 1] if k < NG - 1 else zero
-            under = ts[k - 1] if k > 0 else zero
-            nb.append(e0[k] + corner(k, 1) * over + corner(k, 0) * under)
-            nt.append(e1[k] + corner(k, 3) * over + corner(k, 2) * under)
-        bs, ts = nb, nt
-    for k in range(NG):
-        bpad[pl.ds(k * 16, 16), :] = bs[k]
-        tpad[pl.ds(k * 16 + 16, 16), :] = ts[k]
-    bpad[pl.ds(NG * 16, 16), :] = zero
-    tpad[pl.ds(0, 16), :] = zero
-    over = bpad[pl.ds(pl.multiple_of(g * 16 + 16, 8), 16), :]
-    under = tpad[pl.ds(pl.multiple_of(g * 16, 8), 16), :]
+    for d, there in near:
+        @pl.when(there)
+        def _(d=d):
+            corner_msg(d, g).wait_send()
+            corner_msg(d, g + d).wait_recv()
+            edge_msg(d, g, d).wait_send()
+            edge_msg(d, g + d, -d).wait_recv()
+
+    def e0(d):
+        return edges[pl.ds(pl.multiple_of((g + 3 + d) * 32, 8), 16), :]
+
+    def e1(d):
+        return edges[pl.ds(pl.multiple_of((g + 3 + d) * 32 + 16, 8), 16), :]
+
+    def corner(d, i):
+        return jnp.broadcast_to(corners[pl.ds((g + 3 + d) * 8 + i, 1), :], (16, 128))
+
+    def low_edge(d, over, under):
+        return e0(d) + corner(d, 1) * over + corner(d, 0) * under
+
+    def high_edge(d, over, under):
+        return e1(d) + corner(d, 3) * over + corner(d, 2) * under
+
+    over = low_edge(1, low_edge(2, e0(3), e1(1)), high_edge(0, e0(1), e1(-1)))
+    under = high_edge(-1, low_edge(0, e0(1), e1(-1)), high_edge(-2, e0(-1), e1(-3)))
 
     def update(i, _):
         s = pl.ds(i * 16, 16)
@@ -503,7 +533,7 @@
         c.wait()
 
 
-CUT = (6, 8, 14)
+CUT = (5, 8, 14)
 
 
 def body(bins, u, w, fall, kern, redi, ids, counts, binv):
@@ -519,8 +549,8 @@
             vmem((NL + 1) * LVL), vmem(256), vmem(256), vmem(1024), vmem(480, 256, BF16), vmem(128, 256),
             vmem(NB, NB), vmem(NB, NB), vmem(1, 64, jnp.int32), vmem(1, NB), vmem(1, 1, jnp.int32), vmem(2 * NBP, 3 * NBP), vmem(LVL),
             vmem(512), vmem(512), vmem(512), vmem(512), vmem(512), vmem(512), vmem(256), vmem(256),
-            vmem(32), vmem(NG * 32), vmem(8), vmem(NG * 8), vmem((NG + 1) * 16), vmem((NG + 1) * 16),
-            vmem(8), vmem(LVL), vmem(LVL), vmem(128), vmem(128), vmem(128), vmem(128), vmem(128), vmem(128), vmem(128),
+            vmem(32), vmem((NG + 6) * 32), vmem(8), vmem((NG + 6) * 8),
+            vmem(8), vmem(LVL), vmem(LVL), vmem(128), vmem(128), vmem(128), vmem(128), vmem(128),
             vmem(NBP * 8), vmem(LVL), vmem(8),
             dma((10,)), dma((8,)),
             dma((4, NP)), dma((4, NP)), dma((NG,)), dma((NG,)), dma((NG,)), dma((NG,)), dma((6,)), dma((6,)), dma, dma((NP,)),

time: 56.5 us -> 52.9 us (0.936); the launches traced: 56.4 us -> 52.2 us
  Pallas kernels: 55.1 us -> 50.9 us
    pallas_call x1, Pallas kernels: 53 us -> 48.8 us  [body(): pl.pallas_call(kernel_body, out_shape=(pltpu.VMEM((NL * LVL, 128), F32),...]
where the time goes in v3:
time: 52.9 us; the launch traced here: 52.2 us
  Pallas kernels  50.9 us (96%)
  between operations  1.29 us (2%)
    pallas_call x1, Pallas kernels, body(): pl.pallas_call(kernel_body, out_shape=(pltpu.VMEM((NL * LVL, 128), F32),...  48.8 us
    pallas_call x1, Pallas kernels, body(): pl.pallas_call(write_body, out_shape=(jax.ShapeDtypeStruct((NL * LVL, 128...  2.16 us

profile of v3, /device:TPU:1, one launch (start us, length us, event | category | flops | bytes accessed | tf_op | source)
XLA Modules:
  0.0 52.2 jit_solution(12477287967427463127)
XLA Ops:
  1.3 48.8 %slab_step.1 = (f32[8448,128]{1,0:T(8,128)S(1)}, f32[256,128]{1,0:T(8,128)S(1)}) custom-call(f32[8448,128]{1,0:T(8,128)} %bitcast.7, f32[256,128]{1,0:T(8,128)} %bitcast.9, f32[256,128]{1,0:T(8,128)} %bitcast.10, f32[1024,128]{1,0:T(8,128)} %bitcast.8, bf16[480,256]{1,0:T(8,128)(2,1)} %constant.4.clone.mats_h, f32[128,256]{1,0:T(8,128)} %constant.5.clone.tw_h, ...), custom_call_target="tpu_custom_call" | custom-call | tf_op jit(solution)/shard_map/slab_step/pallas_call | solution.py:543
  50.0 2.2 %write_out.1 = (f32[8448,128]{1,0:T(8,128)}, f32[256,128]{1,0:T(8,128)}) custom-call(f32[8448,128]{1,0:T(8,128)S(1)} %get-tuple-element.6.out_v, f32[256,128]{1,0:T(8,128)S(1)} %get-tuple-element.7.pres_v), custom_call_target="tpu_custom_call" | custom-call | tf_op jit(solution)/shard_map/write_out/pallas_call | solution.py:564

commit v4 on v3

--- a/solution.py
+++ b/solution.py
@@ -122,7 +122,7 @@
         lax.fori_loop(1, NP, greet_low, 0)
 
     bin_loads = [
-        pltpu.make_async_copy(bins_h.at[pl.ds(i * 4 * LVL, 4 * LVL)], bins_v.at[pl.ds(i * 4 * LVL, 4 * LVL)], bin_sem.at[i])
+        pltpu.make_async_copy(bins_h.at[pl.ds(i * 4 * LVL, 4 * LVL)], bins_v.at[pl.ds(i * 4 * LVL, 4 * LVL)], bin_sem)
         for i in range(8)
     ]
     for i in range(8):
@@ -155,7 +155,7 @@
     def w_msg(p):
         return pltpu.make_async_remote_copy(
             src_ref=w_v.at[pl.ds(248, 8)], dst_ref=wtop.at[pl.ds(pl.multiple_of(p * 8, 8), 8)],
-            send_sem=w_send, recv_sem=w_recv.at[p], device_id={"gx": me * 0, "gz": lax.rem(g + 1, NG)}, device_id_type=MESH)
+            send_sem=w_send, recv_sem=w_recv, device_id={"gx": me * 0, "gz": lax.rem(g + 1, NG)}, device_id_type=MESH)
 
     @pl.when(not_last)
     def _():
@@ -166,7 +166,7 @@
         d0 = pl.multiple_of(me * at, 8)
         return pltpu.make_async_remote_copy(
             src_ref=src.at[pl.ds(s0, rows)], dst_ref=dst.at[pl.ds(d0, rows)],
-            send_sem=a2a_send.at[stage, peer], recv_sem=a2a_recv.at[stage, me],
+            send_sem=a2a_send.at[stage], recv_sem=a2a_recv.at[stage],
             device_id={"gx": peer}, device_id_type=MESH)
 
     def send_all(stage, src, dst, rows, at):
@@ -175,16 +175,11 @@
             return 0
         lax.fori_loop(0, NP - 1, step, 0)
 
-    def wait_all(stage, src, dst, rows, at):
-        def step(t, _):
-            peer = lax.rem(me + t + 1, NP)
-            d0 = pl.multiple_of(peer * at, 8)
-            pltpu.make_async_remote_copy(
-                src_ref=src.at[pl.ds(d0, rows)], dst_ref=dst.at[pl.ds(d0, rows)],
-                send_sem=a2a_send.at[stage, peer], recv_sem=a2a_recv.at[stage, peer],
-                device_id={"gx": peer}, device_id_type=MESH).wait()
-            return 0
-        lax.fori_loop(0, NP - 1, step, 0)
+    def wait_all(stage, src, dst, rows):
+        total = pl.ds(0, (NP - 1) * rows)
+        pltpu.make_async_remote_copy(
+            src_ref=src.at[total], dst_ref=dst.at[total], send_sem=a2a_send.at[stage], recv_sem=a2a_recv.at[stage],
+            device_id={"gx": lax.rem(me + 1, NP)}, device_id_type=MESH).wait()
 
     def own(src, dst, rows, at):
         m0 = pl.multiple_of(me * at, 8)
@@ -193,8 +188,7 @@
     send_all(0, send1, x1, 9, 16)
     own(send1, x1, 16, 16)
 
-    bin_loads[7].wait()
-    bin_loads[0].wait()
+    pltpu.make_async_copy(bins_h, bins_v.at[pl.ds(0, NL * LVL)], bin_sem).wait()
     z_up = pltpu.make_async_remote_copy(
         src_ref=bins_v.at[pl.ds(31 * LVL, LVL)], dst_ref=zlo, send_sem=h_send.at[1], recv_sem=h_recv.at[1],
         device_id=above, device_id_type=MESH)
@@ -228,17 +222,17 @@
     for i, r in enumerate((0, 31, 31 * 32, 31 * 32 + 31)):
         csend[pl.ds(i, 1), :] = binv_v[pl.ds(r, 1), :]
 
-    def corner_msg(d, group):
+    def corner_msg(d, group, toward):
         return pltpu.make_async_remote_copy(
             src_ref=csend, dst_ref=corners.at[pl.ds(pl.multiple_of((group + 3) * 8, 8), 8)],
-            send_sem=c_send.at[d + 3], recv_sem=c_recv.at[group], device_id={"gz": lax.rem(g + d + NG, NG)}, device_id_type=MESH)
+            send_sem=c_send.at[d + 3], recv_sem=c_recv.at[toward + 3], device_id={"gz": lax.rem(g + d + NG, NG)}, device_id_type=MESH)
 
     def edge_msg(d, group, toward):
         first = 16 if abs(d) > 1 and toward > 0 else 0
         rows = 32 if abs(d) == 1 else 16
         return pltpu.make_async_remote_copy(
             src_ref=esend.at[pl.ds(first, rows)], dst_ref=edges.at[pl.ds(pl.multiple_of((group + 3) * 32 + first, 8), rows)],
-            send_sem=e_send.at[d + 3], recv_sem=e_recv.at[group], device_id={"gz": lax.rem(g + d + NG, NG)}, device_id_type=MESH)
+            send_sem=e_send.at[d + 3], recv_sem=e_recv.at[toward + 3], device_id={"gz": lax.rem(g + d + NG, NG)}, device_id_type=MESH)
 
     for lo in (0, NG + 3):
         edges[pl.ds(lo * 32, 96), :] = jnp.zeros((96, 128), F32)
@@ -247,10 +241,8 @@
     for d, there in near:
         @pl.when(there)
         def _(d=d):
-            corner_msg(d, g).start()
-
-    for i in range(1, 7):
-        bin_loads[i].wait()
+            corner_msg(d, g, d).start()
+
 
     turned = lax.rem(lane + 1, 128)
 
@@ -353,14 +345,13 @@
             return 0
         lax.fori_loop(first, last, step, 0)
 
-    wait_all(0, send1, x1, 9, 16)
+    wait_all(0, send1, x1, 9)
 
     @pl.when(takes_w)
     def _():
-        def step(p, _):
-            w_msg(p).wait_recv()
-            return 0
-        lax.fori_loop(0, NP, step, 0)
+        pltpu.make_async_remote_copy(
+            src_ref=wtop, dst_ref=wtop, send_sem=w_send, recv_sem=w_recv,
+            device_id={"gx": lax.rem(me + 1, NP)}, device_id_type=MESH).wait_recv()
 
     borders = x1[pl.ds(8, NP, stride=16), :]
     borders = pltpu.roll(borders, 1, 0)
@@ -427,7 +418,7 @@
 
     levels(0, CUT[0])
 
-    wait_all(1, send2, x2, 16, 16)
+    wait_all(1, send2, x2, 16)
 
     def apply_rows(rows):
         accs = [None] * len(rows)
@@ -458,8 +449,8 @@
     for d, there in near:
         @pl.when(there)
         def _(d=d):
-            corner_msg(d, g).wait_send()
-            corner_msg(d, g + d).wait_recv()
+            corner_msg(d, g, d).wait_send()
+            corner_msg(d, g + d, -d).wait_recv()
             edge_msg(d, g, d).wait_send()
             edge_msg(d, g + d, -d).wait_recv()
 
@@ -481,20 +472,22 @@
     over = low_edge(1, low_edge(2, e0(3), e1(1)), high_edge(0, e0(1), e1(-1)))
     under = high_edge(-1, low_edge(0, e0(1), e1(-1)), high_edge(-2, e0(-1), e1(-3)))
 
-    def update(i, _):
-        s = pl.ds(i * 16, 16)
-        top = jnp.broadcast_to(binv_v[pl.ds(i * 32 + 31, 1), :], (16, 128))
-        bot = jnp.broadcast_to(binv_v[pl.ds(i * 32, 1), :], (16, 128))
-        send3[s, :] = send3[s, :] + top * over + bot * under
+    def update(t, _):
+        for n in range(4):
+            i = t * 4 + n
+            s = pl.ds(i * 16, 16)
+            top = jnp.broadcast_to(binv_v[pl.ds(i * 32 + 31, 1), :], (16, 128))
+            bot = jnp.broadcast_to(binv_v[pl.ds(i * 32, 1), :], (16, 128))
+            send3[s, :] = send3[s, :] + top * over + bot * under
         return 0
 
-    lax.fori_loop(0, NL, update, 0)
+    lax.fori_loop(0, NL // 4, update, 0)
     send_all(2, send3, x3, 16, 16)
     own(send3, x3, 16, 16)
 
     levels(CUT[1], CUT[2])
 
-    wait_all(2, send3, x3, 16, 16)
+    wait_all(2, send3, x3, 16)
     g3 = mats_v[pl.ds(224, 192), :]
     h2 = mats_v[pl.ds(416, 64), :]
     for h in range(4):
@@ -519,7 +512,7 @@
     def _():
         w_msg(me).wait_send()
 
-    wait_all(3, send4, pres_v, 8, 8)
+    wait_all(3, send4, pres_v, 8)
 
 
 def write_body(out_v, pres_v, out_h, pres_h, sem):
@@ -552,8 +545,8 @@
             vmem(32), vmem((NG + 6) * 32), vmem(8), vmem((NG + 6) * 8),
             vmem(8), vmem(LVL), vmem(LVL), vmem(128), vmem(128), vmem(128), vmem(128), vmem(128),
             vmem(NBP * 8), vmem(LVL), vmem(8),
-            dma((10,)), dma((8,)),
-            dma((4, NP)), dma((4, NP)), dma((NG,)), dma((NG,)), dma((NG,)), dma((NG,)), dma((6,)), dma((6,)), dma, dma((NP,)),
+            dma((10,)), dma,
+            dma((4,)), dma((4,)), dma((7,)), dma((7,)), dma((7,)), dma((7,)), dma((5,)), dma((5,)), dma, dma,
         ],
         compiler_params=pltpu.CompilerParams(collective_id=0, has_side_effects=True, vmem_limit_bytes=62300000),
         name="slab_step",

time: 52.9 us -> 49.4 us (0.934); the launches traced: 52.2 us -> 49.3 us
  Pallas kernels: 50.9 us -> 48 us
    pallas_call x1, Pallas kernels: 48.8 us -> 45.9 us  [body(): pl.pallas_call(kernel_body, out_shape=(pltpu.VMEM((NL * LVL, 128), F32),...]
where the time goes in v4:
time: 49.4 us; the launch traced here: 49.3 us
  Pallas kernels  48 us (97%)
  between operations  1.29 us (3%)
    pallas_call x1, Pallas kernels, body(): pl.pallas_call(kernel_body, out_shape=(pltpu.VMEM((NL * LVL, 128), F32),...  45.9 us
    pallas_call x1, Pallas kernels, body(): pl.pallas_call(write_body, out_shape=(jax.ShapeDtypeStruct((NL * LVL, 128...  2.16 us

profile of v4, /device:TPU:1, one launch (start us, length us, event | category | flops | bytes accessed | tf_op | source)
XLA Modules:
  0.0 49.3 jit_solution(5235775790688647430)
XLA Ops:
  1.3 45.9 %slab_step.1 = (f32[8448,128]{1,0:T(8,128)S(1)}, f32[256,128]{1,0:T(8,128)S(1)}) custom-call(f32[8448,128]{1,0:T(8,128)} %bitcast.7, f32[256,128]{1,0:T(8,128)} %bitcast.9, f32[256,128]{1,0:T(8,128)} %bitcast.10, f32[1024,128]{1,0:T(8,128)} %bitcast.8, bf16[480,256]{1,0:T(8,128)(2,1)} %constant.4.clone.mats_h, f32[128,256]{1,0:T(8,128)} %constant.5.clone.tw_h, ...), custom_call_target="tpu_custom_call" | custom-call | tf_op jit(solution)/shard_map/slab_step/pallas_call | solution.py:536
  47.1 2.2 %write_out.1 = (f32[8448,128]{1,0:T(8,128)}, f32[256,128]{1,0:T(8,128)}) custom-call(f32[8448,128]{1,0:T(8,128)S(1)} %get-tuple-element.6.out_v, f32[256,128]{1,0:T(8,128)S(1)} %get-tuple-element.7.pres_v), custom_call_target="tpu_custom_call" | custom-call | tf_op jit(solution)/shard_map/write_out/pallas_call | solution.py:557

commit v5 on v4

--- a/solution.py
+++ b/solution.py
@@ -203,10 +203,6 @@
     def _():
         w_up.start()
         z_up.start()
-
-    @pl.when(not_first)
-    def _():
-        z_down.start()
 
     @pl.when(jnp.logical_not(not_first))
     def _():
@@ -384,13 +380,11 @@
     def _():
         z_up.wait_send()
         w_up.wait_send()
-        z_down.wait_recv()
 
     @pl.when(not_first)
     def _():
         z_up.wait_recv()
         w_up.wait_recv()
-        z_down.wait_send()
 
     for c in x_copies:
         c.wait()
@@ -410,7 +404,6 @@
         s = pl.ds(m * 8, 8)
         c = w_low - fall_t[s, :]
         fz[s, :] = jnp.maximum(c, 0.0) * jnp.where(not_first, zlo[s, :], 0.0) + jnp.minimum(c, 0.0) * bins_v[s, :]
-        bins_v[pl.ds(NL * LVL + m * 8, 8), :] = jnp.where(not_last, zhi[s, :], 0.0)
         return 0
 
     lax.fori_loop(0, NB, low_face, 0)
@@ -445,6 +438,10 @@
         return 0
 
     lax.fori_loop(0, NL // 4, solve_step, 0)
+    @pl.when(not_first)
+    def _():
+        z_down.start()
+
     levels(CUT[0], CUT[1])
     for d, there in near:
         @pl.when(there)
@@ -506,6 +503,20 @@
     send_all(3, send4, pres_v, 8, 8)
     own(send4, pres_v, 8, 8)
 
+    @pl.when(not_last)
+    def _():
+        z_down.wait_recv()
+
+    @pl.when(not_first)
+    def _():
+        z_down.wait_send()
+
+    def top_level(m, _):
+        s = pl.ds(m * 8, 8)
+        bins_v[pl.ds(NL * LVL + m * 8, 8), :] = jnp.where(not_last, zhi[s, :], 0.0)
+        return 0
+
+    lax.fori_loop(0, NB, top_level, 0)
     levels(CUT[2], NL // 2)
 
     @pl.when(not_last)

time: 49.4 us -> 49.4 us (level)
  no operation moved by 1% of the time
where the time goes in v5:
time: 49.4 us; the launch traced here: 49.3 us
  Pallas kernels  48 us (97%)
  between operations  1.29 us (3%)
    pallas_call x1, Pallas kernels, body(): pl.pallas_call(kernel_body, out_shape=(pltpu.VMEM((NL * LVL, 128), F32),...  45.8 us
    pallas_call x1, Pallas kernels, body(): pl.pallas_call(write_body, out_shape=(jax.ShapeDtypeStruct((NL * LVL, 128...  2.16 us

profile of v5, /device:TPU:1, one launch (start us, length us, event | category | flops | bytes accessed | tf_op | source)
XLA Modules:
  0.0 49.3 jit_solution(6981088872986296973)
XLA Ops:
  1.3 45.8 %slab_step.1 = (f32[8448,128]{1,0:T(8,128)S(1)}, f32[256,128]{1,0:T(8,128)S(1)}) custom-call(f32[8448,128]{1,0:T(8,128)} %bitcast.7, f32[256,128]{1,0:T(8,128)} %bitcast.9, f32[256,128]{1,0:T(8,128)} %bitcast.10, f32[1024,128]{1,0:T(8,128)} %bitcast.8, bf16[480,256]{1,0:T(8,128)(2,1)} %constant.4.clone.mats_h, f32[128,256]{1,0:T(8,128)} %constant.5.clone.tw_h, ...), custom_call_target="tpu_custom_call" | custom-call | tf_op jit(solution)/shard_map/slab_step/pallas_call | solution.py:547
  47.1 2.2 %write_out.1 = (f32[8448,128]{1,0:T(8,128)}, f32[256,128]{1,0:T(8,128)}) custom-call(f32[8448,128]{1,0:T(8,128)S(1)} %get-tuple-element.6.out_v, f32[256,128]{1,0:T(8,128)S(1)} %get-tuple-element.7.pres_v), custom_call_target="tpu_custom_call" | custom-call | tf_op jit(solution)/shard_map/write_out/pallas_call | solution.py:568
